TPU v7x, 32 devices: a whole 2x2x4 slice. The times are simulated.
32 devices in a mesh: seq: 2 (over y), row: 4 (over x, core), col: 4 (over z).
Axes of the slice: x: 2, y: 2, z: 4, core: 2. Of those that a mesh axis runs over, the one named last changes fastest.
Arguments:
- tokens: bfloat16 [4096, 5376], P(('seq', 'row'), 'col'), may hold values from -6 to 6
- w_query: bfloat16 [5376, 4096], P(('seq', 'row'), 'col'), may hold values from -0.078125 to 0.078125
- key_weight: bfloat16 [5376, 2048], P(('seq', 'row'), 'col'), may hold values from -0.078125 to 0.078125
- value_weight: bfloat16 [5376, 2048], P(('seq', 'row'), 'col'), may hold values from -0.078125 to 0.078125
- w_output: bfloat16 [4096, 5376], P(('seq', 'row'), 'col'), may hold values from -0.09375 to 0.09375
- query_gain: float32 [128], replicated, may hold values from 0.5 to 8
- key_gain: float32 [128], replicated, may hold values from 0.5 to 8
Outputs:
- attended: bfloat16 [4096, 5376], P(('seq', 'row'), 'col')
All inputs are finite; a program needn't handle non-finite values.
Results may differ from a plain program's by a relative error of at most 0.0085.
The roundings to bfloat16 on the way count: a program that leaves them out, or rounds other values in their place, can miss the bound.
Values may be sent and summed in bfloat16 or wider, within the bound.
A program may use at most 128 MiB of HBM per device.

v0:
```python
import jax
import jax.numpy as jnp
from jax import lax
from jax.sharding import PartitionSpec as P

HEAD_SIZE = 128
WINDOW_KEYS = 1024
query_scale = 168.0 ** (-0.5)


def shifted(block, axis, distance):
    devices = range(lax.axis_size(axis))
    route = [(i - distance, i) for i in devices if i - distance in devices]
    return lax.ppermute(block, axis, route)


def head_norm(block, gain):
    mean_square = jnp.mean(block * block, axis=-1, keepdims=True)
    return block * lax.rsqrt(mean_square + 1e-06) * gain


def rotate(block, positions):
    half = block.shape[-1] // 2
    freqs = 10000.0 ** (-(jnp.arange(half, dtype=jnp.float32) * 2.0 / block.shape[-1]))
    angles = positions.astype(jnp.float32)[:, None] * freqs[None, :]
    cosine = jnp.cos(angles)[:, None, :]
    sine = jnp.sin(angles)[:, None, :]
    first = block[..., :half]
    second = block[..., half:]
    return jnp.concatenate(
        [first * cosine - second * sine, second * cosine + first * sine], axis=-1
    )


def attend(queries, key_states, value_states, qpos, kpos):
    rows = queries.shape[0]
    kv_heads = key_states.shape[1]
    grouped = queries.reshape(rows, kv_heads, 2, HEAD_SIZE)
    scores = (
        jnp.einsum("bhgd,khd->hgbk", grouped, key_states, preferred_element_type=jnp.float32)
        * query_scale
    )
    gap = qpos[:, None] - kpos[None, :]
    valid = (kpos[None, :] >= 0) & (gap >= 0) & (gap < WINDOW_KEYS)
    scores = jnp.where(valid[None, None], scores, -1e30)
    top = jnp.max(scores, axis=-1, keepdims=True)
    weights = jnp.exp(scores - top)
    weights = (weights / jnp.sum(weights, axis=-1, keepdims=True)).astype(jnp.bfloat16)
    mixed = jnp.einsum("hgbk,khd->bhgd", weights, value_states, preferred_element_type=jnp.float32)
    return mixed.astype(jnp.bfloat16).reshape(rows, kv_heads * 2 * HEAD_SIZE)


def shards(tokens, w_query, key_weight, value_weight, w_output, query_gain, key_gain):
    rows = tokens.shape[0]
    whole = lax.all_gather(tokens, "col", axis=1, tiled=True)
    columns = whole
    proj_q = jnp.dot(
        columns,
        lax.all_gather(w_query, ("seq", "row"), axis=0, tiled=True),
        preferred_element_type=jnp.float32,
    )
    projected_key = jnp.dot(
        columns,
        lax.all_gather(key_weight, ("seq", "row"), axis=0, tiled=True),
        preferred_element_type=jnp.float32,
    )
    proj_v = jnp.dot(
        columns,
        lax.all_gather(value_weight, ("seq", "row"), axis=0, tiled=True),
        preferred_element_type=jnp.float32,
    )
    base = lax.axis_index(("seq", "row")) * rows
    positions = base + jnp.arange(rows, dtype=jnp.int32)
    q_heads = proj_q.shape[1] // HEAD_SIZE
    kv_heads = projected_key.shape[1] // HEAD_SIZE
    queries = rotate(
        head_norm(proj_q.reshape(rows, q_heads, HEAD_SIZE), query_gain), positions
    ).astype(jnp.bfloat16)
    key_states = rotate(
        head_norm(projected_key.reshape(rows, kv_heads, HEAD_SIZE), key_gain), positions
    ).astype(jnp.bfloat16)
    key_flat = key_states.reshape(rows, kv_heads * HEAD_SIZE)
    value_flat = proj_v.astype(jnp.bfloat16)
    prior_one = shifted((key_flat, value_flat), ("seq", "row"), 1)
    prior_two = shifted((key_flat, value_flat), ("seq", "row"), 2)
    key_rows = jnp.concatenate([prior_two[0], prior_one[0], key_flat], axis=0).reshape(
        3 * rows, kv_heads, HEAD_SIZE
    )
    value_rows = jnp.concatenate([prior_two[1], prior_one[1], value_flat], axis=0).reshape(
        3 * rows, kv_heads, HEAD_SIZE
    )
    kpos = base - 2 * rows + jnp.arange(3 * rows, dtype=jnp.int32)
    mixed = attend(queries, key_rows, value_rows, positions, kpos)
    all_heads = lax.all_gather(mixed, "col", axis=1, tiled=True)
    columns = all_heads
    attended = jnp.dot(
        columns,
        lax.all_gather(w_output, ("seq", "row"), axis=0, tiled=True),
        preferred_element_type=jnp.float32,
    )
    return attended.astype(jnp.bfloat16)


def solution(mesh):
    return jax.shard_map(
        shards,
        mesh=mesh,
        in_specs=(
            P(("seq", "row"), "col"),
            P(("seq", "row"), "col"),
            P(("seq", "row"), "col"),
            P(("seq", "row"), "col"),
            P(("seq", "row"), "col"),
            P(),
            P(),
        ),
        out_specs=P(("seq", "row"), "col"),
        check_vma=False,
    )
```

profile of v0, /device:TPU:0, one launch (start us, length us, event | category | flops | bytes accessed | tf_op | source)
XLA Modules:
  0.0 458.2 jit_solution(17075732382961147357)
XLA Ops:
  6.5 0.7 all-gather.7.cloned.1.call-update
  7.3 0.7 all-gather.11.cloned.1.call-update
  8.1 0.7 all-gather.9.cloned.1.call-update
  9.4 0.5 all-gather.17.cloned.1.call-update
  10.0 1.0 multiply_cosine_fusion
  11.0 103.0 %all-gather.7.cloned.1.call-done = bf16[512,5376]{0,1:T(8,128)(2,1)} async-done(((bf16[512,1344]{0,1:T(8,128)(2,1)}), bf16[512,5376]{0,1:T(8,128)(2,1)}) %all-gather.7.cloned.1.call-update) | async-done | bytes 5505040 | tf_op jit(solution)/shard_map/all_gather | solution.py:55
  114.0 42.5 %all-gather.11.cloned.1.call-done = bf16[5376,512]{1,0:T(8,128)(2,1)} async-done(((bf16[672,512]{1,0:T(8,128)(2,1)}), bf16[5376,512]{1,0:T(8,128)(2,1)}) %all-gather.11.cloned.1.call-update) | async-done | bytes 5505040 | tf_op jit(solution)/shard_map/all_gather | solution.py:64
  156.5 6.7 %multiply_reduce_fusion.1 = (f32[512,4]{0,1:T(4,128)S(1)}, f32[512,512]{0,1:T(8,128)S(1)}) fusion(bf16[512,5376]{0,1:T(8,128)(2,1)} %all-gather.7.cloned.1.call-done, bf16[5376,512]{1,0:T(8,128)(2,1)} %all-gather.11.cloned.1.call-done), kind=kOutput, calls=%fused_computation.29 | convolution fusion | flops 2819094528 | bytes 12066816 | tf_op jit(solution)/shard_map/dot_general | solution.py:62
  164.9 3.4 collective-permute-start.2
  168.3 1.9 collective-permute-start.3
  170.3 39.0 %all-gather.9.cloned.1.call-done = bf16[5376,512]{1,0:T(8,128)(2,1)} async-done(((bf16[672,512]{1,0:T(8,128)(2,1)}), bf16[5376,512]{1,0:T(8,128)(2,1)}) %all-gather.9.cloned.1.call-update) | async-done | bytes 5505040 | tf_op jit(solution)/shard_map/all_gather | solution.py:69
  209.3 7.2 %convolution_convert_fusion.1 = bf16[512,512]{1,0:T(8,128)(2,1)S(1)} fusion(bf16[512,5376]{0,1:T(8,128)(2,1)} %all-gather.7.cloned.1.call-done, bf16[5376,512]{1,0:T(8,128)(2,1)} %all-gather.9.cloned.1.call-done), kind=kOutput, calls=%fused_computation.23 | convolution fusion | flops 2818834432 | bytes 11534336 | tf_op jit(solution)/shard_map/dot_general | solution.py:67
  216.5 3.1 collective-permute-start
  219.6 2.7 collective-permute-start.1
  222.2 2.0 fusion.9
  224.2 1.0 copy.32
  225.2 1.0 copy.33
  226.2 15.8 %collective-permute-done = bf16[512,512]{1,0:T(8,128)(2,1)} collective-permute-done((bf16[512,512]{1,0:T(8,128)(2,1)S(1)}, bf16[512,512]{1,0:T(8,128)(2,1)}, u32[]{:S(2)}, u32[]{:S(2)}) %collective-permute-start) | collective-permute-done | bytes 524320 | tf_op jit(solution)/shard_map/ppermute | solution.py:14
  242.0 1.3 pad_maximum_fusion
  243.3 1.6 copy.43
  244.9 44.2 %all-gather.13.cloned.1.call-done = bf16[5376,1024]{1,0:T(8,128)(2,1)} async-done(((bf16[672,1024]{1,0:T(8,128)(2,1)}), bf16[5376,1024]{1,0:T(8,128)(2,1)}) %all-gather.13.cloned.1.call-update) | async-done | bytes 11010064 | tf_op jit(solution)/shard_map/all_gather | solution.py:59
  289.1 10.3 %convolution_bitcast_fusion = f32[64,8,8,128]{3,1,2,0:T(8,128)S(1)} fusion(bf16[512,5376]{0,1:T(8,128)(2,1)} %all-gather.7.cloned.1.call-done, bf16[5376,1024]{1,0:T(8,128)(2,1)} %all-gather.13.cloned.1.call-done), kind=kOutput, calls=%fused_computation.19 | convolution fusion | flops 5637144576 | bytes 18612224 | tf_op jit(solution)/shard_map/dot_general | solution.py:57
  299.9 0.6 multiply_reduce_fusion
  300.8 0.9 multiply_multiply_fusion
  301.6 0.9 subtract_convert_fusion
  302.8 0.7 copy-done
  303.7 11.8 %fusion.11 = f32[4,1536,512,2]{2,1,3,0:T(8,128)} fusion(bf16[512,4,128]{2,0,1:T(8,128)(2,1)S(1)} %maximum_convert_fusion, bf16[512,4,128]{2,0,1:T(8,128)(2,1)S(1)} %copy-done.1, bf16[512,4,128]{2,0,1:T(8,128)(2,1)S(1)} %copy-done, bf16[512,4,2,64]{3,0,2,1:T(8,128)(2,1)S(1)} %bitcast.51, bf16[512,4,2,64]{3,0,2,1:T(8,128)(2,1)S(1)} %bitcast.53), kind=kOutput, calls=%fused_computation.30 | convolution fusion | flops 1617428480 | bytes 27787264 | tf_op jit(solution)/shard_map/bhgd,khd->hgbk/dot_general | solution.py:40
  315.6 10.5 %fusion.23 = f32[4,2,512]{2,1,0:T(2,128)S(1)} fusion(pred[512,1536]{0,1:T(8,128)(4,1)} %fusion.9, bf16[512,4,128]{2,0,1:T(8,128)(2,1)S(1)} %maximum_convert_fusion, bf16[512,4,128]{2,0,1:T(8,128)(2,1)} %copy.33, bf16[512,4,128]{2,0,1:T(8,128)(2,1)S(1)} %copy-done, bf16[512,4,2,64]{3,0,2,1:T(8,128)(2,1)S(1)} %bitcast.52, bf16[512,4,2,64]{3,0,2,1:T(8,128)(2,1)S(1)} %bitcast.54), kind=kOutput, calls=%fused_computation.47 | convolution fusion | flops 1642595840 | bytes 3424256 | tf_op jit(solution)/shard_map/sub | solution.py:47
  326.1 15.4 %fusion.10 = bf16[4,128,2,512]{3,1,2,0:T(8,128)(2,1)} fusion(bf16[1536,4,128,1]{0,2,3,1:T(8,128)(2,1)} %bitcast.55, f32[4,2,512]{2,1,0:T(2,128)S(1)} %fusion.23, f32[4,1536,512,2]{2,1,3,0:T(8,128)} %fusion.11, pred[512,1536]{0,1:T(8,128)(4,1)} %fusion.9), kind=kOutput, calls=%fused_computation.22 | convolution fusion | flops 1642599936 | bytes 28590080 | tf_op jit(solution)/shard_map/hgbk,khd->bhgd/dot_general | solution.py:49
  341.5 17.0 %all-gather.17.cloned.1.call-done = bf16[4096,1344]{0,1:T(8,128)(2,1)} async-done(((bf16[512,1344]{0,1:T(8,128)(2,1)}), bf16[4096,1344]{0,1:T(8,128)(2,1)}) %all-gather.17.cloned.1.call-update) | async-done | bytes 11010064 | tf_op jit(solution)/shard_map/all_gather | solution.py:98
  358.5 82.2 %all-gather.15.cloned.1.call-done = bf16[512,4096]{0,1:T(8,128)(2,1)} async-done(((bf16[512,1024]{0,1:T(8,128)(2,1)}), bf16[512,4096]{0,1:T(8,128)(2,1)}) %all-gather.15.cloned.1.call-update) | async-done | bytes 4194320 | tf_op jit(solution)/shard_map/all_gather | solution.py:94
  440.7 10.7 %convolution_convert_fusion = bf16[512,1344]{0,1:T(8,128)(2,1)} fusion(bf16[4096,1344]{0,1:T(8,128)(2,1)} %all-gather.17.cloned.1.call-done, bf16[512,4096]{0,1:T(8,128)(2,1)} %all-gather.15.cloned.1.call-done), kind=kOutput, calls=%fused_computation.14 | convolution fusion | flops 5637832704 | bytes 16580608 | tf_op jit(solution)/shard_map/dot_general | solution.py:96
  (35 shorter events, 3.6 us)
Async XLA Ops:
  6.5 107.5 %all-gather.7.cloned.1.call-start = ((), (), s32[]{:S(2)}) async-start(), calls=%async_computation | async-start | bytes 6881280 | tf_op jit(solution)/shard_map/all_gather | solution.py:55
  7.3 149.3 %all-gather.11.cloned.1.call-start = ((), (), s32[]{:S(2)}) async-start(), calls=%async_computation.2 | async-start | bytes 6193152 | tf_op jit(solution)/shard_map/all_gather | solution.py:64
  8.0 201.3 %all-gather.9.cloned.1.call-start = ((), (), s32[]{:S(2)}) async-start(), calls=%async_computation.1 | async-start | bytes 6193152 | tf_op jit(solution)/shard_map/all_gather | solution.py:69
  8.7 280.4 %all-gather.13.cloned.1.call-start = ((), (), s32[]{:S(2)}) async-start(), calls=%async_computation.3 | async-start | bytes 12386304 | tf_op jit(solution)/shard_map/all_gather | solution.py:59
  9.3 349.2 %all-gather.17.cloned.1.call-start = ((), (), s32[]{:S(2)}) async-start(), calls=%async_computation.5 | async-start | bytes 12386304 | tf_op jit(solution)/shard_map/all_gather | solution.py:98
  9.9 430.8 %all-gather.15.cloned.1.call-start = ((), (), s32[]{:S(2)}) async-start(), calls=%async_computation.4 | async-start | bytes 5242880 | tf_op jit(solution)/shard_map/all_gather | solution.py:94
  11.0 152.6 %copy-start.2 = (f32[128]{0:T(128)S(1)}, f32[128]{0:T(128)}, u32[]{:S(2)}) copy-start(f32[128]{0:T(128)} %param.13) | copy-start | bytes 1540
  164.9 59.3 %collective-permute-start.2 = (bf16[512,512]{0,1:T(8,128)(2,1)S(1)}, bf16[512,512]{0,1:T(8,128)(2,1)S(1)}, u32[]{:S(2)}, u32[]{:S(2)}) collective-permute-start(bf16[512,512]{0,1:T(8,128)(2,1)S(1)} %bitcast.58), channel_id=1, source_target_pairs={{0,8},{4,12},{8,16},{12,20},{16,24},{20,28},{1,9},{5,13},{9,17},{1... | collective-permute-start | bytes 1572872 | tf_op jit(solution)/shard_map/ppermute | solution.py:14
  168.3 56.9 %collective-permute-start.3 = (bf16[512,512]{0,1:T(8,128)(2,1)S(1)}, bf16[512,512]{0,1:T(8,128)(2,1)S(1)}, u32[]{:S(2)}, u32[]{:S(2)}) collective-permute-start(bf16[512,512]{0,1:T(8,128)(2,1)S(1)} %bitcast.59), channel_id=1, source_target_pairs={{0,4},{4,8},{8,12},{12,16},{16,20},{20,24},{24,28},{1,5},{5,9},{9,... | collective-permute-start | bytes 1572872 | tf_op jit(solution)/shard_map/ppermute | solution.py:14
  216.5 25.5 %collective-permute-start = (bf16[512,512]{1,0:T(8,128)(2,1)S(1)}, bf16[512,512]{1,0:T(8,128)(2,1)}, u32[]{:S(2)}, u32[]{:S(2)}) collective-permute-start(bf16[512,512]{1,0:T(8,128)(2,1)S(1)} %convolution_convert_fusion.1), channel_id=1, source_target_pairs={{0,8},{4,12},{8,16},{12,20},{16,24},{20,28},{1,9},{5,13},{9,17},{1... | collective-permute-start | bytes 1572872 | tf_op jit(solution)/shard_map/ppermute | solution.py:14
  219.6 22.5 %collective-permute-start.1 = (bf16[512,512]{1,0:T(8,128)(2,1)S(1)}, bf16[512,512]{1,0:T(8,128)(2,1)}, u32[]{:S(2)}, u32[]{:S(2)}) collective-permute-start(bf16[512,512]{1,0:T(8,128)(2,1)S(1)} %convolution_convert_fusion.1), channel_id=1, source_target_pairs={{0,4},{4,8},{8,12},{12,16},{16,20},{20,24},{24,28},{1,5},{5,9},{9,... | collective-permute-start | bytes 1572872 | tf_op jit(solution)/shard_map/ppermute | solution.py:14
  299.4 1.4 copy-start.3
  302.5 1.1 copy-start
  302.5 1.2 copy-start.1
Sparse Core Ops, SparseCore 0:
  8.9 105.0 all-gather.6
  115.9 40.5 all-gather.10
  158.4 50.8 all-gather.8
  211.0 78.0 all-gather.12
  290.8 67.6 all-gather.16
  359.9 80.7 all-gather.14
where the time goes:
time: 458 us
  waiting for transfers between devices  347 us (76%)
  matrix products  72.6 us (16%)
  between operations  13.7 us (3%)
  starting transfers between devices  11.2 us (2%)
  other arithmetic  7.75 us (2%)
  local copies, waits for them, and re-layouts  6.03 us (1%)
    all_gather x1, waiting for transfers between devices, shards(): whole = lax.all_gather(tokens, 'col', axis=1, tiled=True)  103 us
    all_gather x1, waiting for transfers between devices, shards(): all_heads = lax.all_gather(mixed, 'col', axis=1, tiled=True)  82.2 us
    all_gather x1, waiting for transfers between devices, shards(): lax.all_gather(w_query, ('seq', 'row'), axis=0, tiled=True)  44.2 us
    all_gather x1, waiting for transfers between devices, shards(): lax.all_gather(key_weight, ('seq', 'row'), axis=0, tiled=True)  42.5 us
    all_gather x1, waiting for transfers between devices, shards(): lax.all_gather(value_weight, ('seq', 'row'), axis=0, tiled=True)  39 us
    all_gather x1, waiting for transfers between devices, shards(): lax.all_gather(w_output, ('seq', 'row'), axis=0, tiled=True)  17 us
    ppermute x4, waiting for transfers between devices, shifted(): return lax.ppermute(block, axis, route)  15.8 us
    dot_general x1, matrix products, attend(): jnp.einsum('hgbk,khd->bhgd', weights, value_states, preferred_element_typ...  15.4 us
  transfers between devices with their start and end apart: 10, of which 7 were waited for; matrix products, arithmetic and copies ran while one was open for 16% of the time, Pallas kernels for 0%

commit v1 on v0

--- a/solution.py
+++ b/solution.py
@@ -6,6 +6,17 @@
 HEAD_SIZE = 128
 WINDOW_KEYS = 1024
 query_scale = 168.0 ** (-0.5)
+
+
+def collect(shard, axis, dim):
+    ways = lax.axis_size(axis)
+    pieces = [shard]
+    for far in range(1, ways):
+        pieces.append(
+            lax.ppermute(pieces[far - 1], axis, [(d, (d - 1) % ways) for d in range(ways)])
+        )
+    line = jnp.concatenate(pieces, axis=dim)
+    return jnp.roll(line, lax.axis_index(axis) * shard.shape[dim], axis=dim)
 
 
 def shifted(block, axis, distance):
@@ -65,9 +76,7 @@
         preferred_element_type=jnp.float32,
     )
     proj_v = jnp.dot(
-        columns,
-        lax.all_gather(value_weight, ("seq", "row"), axis=0, tiled=True),
-        preferred_element_type=jnp.float32,
+        columns, collect(value_weight, ("seq", "row"), 0), preferred_element_type=jnp.float32
     )
     base = lax.axis_index(("seq", "row")) * rows
     positions = base + jnp.arange(rows, dtype=jnp.int32)

time: 458 us -> 414 us (0.904)
  waiting for transfers between devices: 347 us -> 261 us
  starting transfers between devices: 11.2 us -> 34.8 us
  local copies, waits for them, and re-layouts: 6.03 us -> 22.8 us
    all_gather x1, waiting for transfers between devices: 103 us -> 14.9 us  [shards(): whole = lax.all_gather(tokens, 'col', axis=1, tiled=True)]
    ppermute x0 -> x7, waiting for transfers between devices: none -> 50.2 us  [collect(): lax.ppermute(pieces[far - 1], axis, [(d, (d - 1) % ways) for d in range(w...]
    all_gather x1 -> x0, waiting for transfers between devices: 39 us -> none  [shards(): lax.all_gather(value_weight, ('seq', 'row'), axis=0, tiled=True)]
    ppermute x0 -> x7, starting transfers between devices: none -> 22.1 us  [collect(): lax.ppermute(pieces[far - 1], axis, [(d, (d - 1) % ways) for d in range(w...]
    unnamed x9 -> x32, local copies, waits for them, and re-layouts: 1.4 us -> 15.2 us
    all_gather x1, waiting for transfers between devices: 42.5 us -> 36.2 us  [shards(): lax.all_gather(key_weight, ('seq', 'row'), axis=0, tiled=True)]
  transfers between devices with their start and end apart: 10 -> 16, of which waited for: 7 -> 13; matrix products, arithmetic and copies ran while one was open for 16% -> 23% of each run, Pallas kernels for 0% -> 0%
where the time goes in v1:
time: 414 us
  waiting for transfers between devices  261 us (63%)
  matrix products  73.8 us (18%)
  starting transfers between devices  34.8 us (8%)
  local copies, waits for them, and re-layouts  22.8 us (6%)
  between operations  13.4 us (3%)
  other arithmetic  8.69 us (2%)
    all_gather x1, waiting for transfers between devices, shards(): all_heads = lax.all_gather(mixed, 'col', axis=1, tiled=True)  82.2 us
    ppermute x7, waiting for transfers between devices, collect(): lax.ppermute(pieces[far - 1], axis, [(d, (d - 1) % ways) for d in range(w...  50.2 us
    all_gather x1, waiting for transfers between devices, shards(): lax.all_gather(w_query, ('seq', 'row'), axis=0, tiled=True)  42.4 us
    all_gather x1, waiting for transfers between devices, shards(): lax.all_gather(key_weight, ('seq', 'row'), axis=0, tiled=True)  36.2 us
    ppermute x7, starting transfers between devices, collect(): lax.ppermute(pieces[far - 1], axis, [(d, (d - 1) % ways) for d in range(w...  22.1 us
    all_gather x1, waiting for transfers between devices, shards(): lax.all_gather(w_output, ('seq', 'row'), axis=0, tiled=True)  17.6 us
    dot_general x1, matrix products, attend(): jnp.einsum('hgbk,khd->bhgd', weights, value_states, preferred_element_typ...  15.4 us
    unnamed x32, local copies, waits for them, and re-layouts  15.2 us
  transfers between devices with their start and end apart: 16, of which 13 were waited for; matrix products, arithmetic and copies ran while one was open for 23% of the time, Pallas kernels for 0%

profile of v1, /device:TPU:0, one launch (start us, length us, event | category | flops | bytes accessed | tf_op | source)
XLA Modules:
  0.0 414.1 jit_solution(15199809862116908650)
XLA Ops:
  9.4 3.4 collective-permute-start
  12.7 8.8 %collective-permute-done = bf16[672,512]{1,0:T(8,128)(2,1)S(1)} collective-permute-done((bf16[672,512]{1,0:T(8,128)(2,1)}, bf16[672,512]{1,0:T(8,128)(2,1)S(1)}, u32[]{:S(2)}, u32[]{:S(2)}) %collective-permute-start) | collective-permute-done | bytes 688160 | tf_op jit(solution)/shard_map/ppermute | solution.py:16
  21.5 2.7 collective-permute-start.1
  24.2 8.5 %collective-permute-done.1 = bf16[672,512]{1,0:T(8,128)(2,1)S(1)} collective-permute-done((bf16[672,512]{1,0:T(8,128)(2,1)S(1)}, bf16[672,512]{1,0:T(8,128)(2,1)S(1)}, u32[]{:S(2)}, u32[]{:S(2)}) %collective-permute-start.1) | collective-permute-done | bytes 688160 | tf_op jit(solution)/shard_map/ppermute | solution.py:16
  32.7 3.2 collective-permute-start.2
  35.9 8.5 %collective-permute-done.2 = bf16[672,512]{1,0:T(8,128)(2,1)S(1)} collective-permute-done((bf16[672,512]{1,0:T(8,128)(2,1)S(1)}, bf16[672,512]{1,0:T(8,128)(2,1)S(1)}, u32[]{:S(2)}, u32[]{:S(2)}) %collective-permute-start.2) | collective-permute-done | bytes 688160 | tf_op jit(solution)/shard_map/ppermute | solution.py:16
  44.3 3.2 collective-permute-start.3
  47.5 8.5 %collective-permute-done.3 = bf16[672,512]{1,0:T(8,128)(2,1)S(1)} collective-permute-done((bf16[672,512]{1,0:T(8,128)(2,1)S(1)}, bf16[672,512]{1,0:T(8,128)(2,1)S(1)}, u32[]{:S(2)}, u32[]{:S(2)}) %collective-permute-start.3) | collective-permute-done | bytes 688160 | tf_op jit(solution)/shard_map/ppermute | solution.py:16
  56.0 3.2 collective-permute-start.4
  59.2 8.4 %collective-permute-done.4 = bf16[672,512]{1,0:T(8,128)(2,1)S(1)} collective-permute-done((bf16[672,512]{1,0:T(8,128)(2,1)S(1)}, bf16[672,512]{1,0:T(8,128)(2,1)S(1)}, u32[]{:S(2)}, u32[]{:S(2)}) %collective-permute-start.4) | collective-permute-done | bytes 688160 | tf_op jit(solution)/shard_map/ppermute | solution.py:16
  67.7 3.2 collective-permute-start.5
  70.9 2.0 constant_dynamic-update-slice_fusion.15
  74.8 4.6 %collective-permute-done.5 = bf16[672,512]{1,0:T(8,128)(2,1)S(1)} collective-permute-done((bf16[672,512]{1,0:T(8,128)(2,1)S(1)}, bf16[672,512]{1,0:T(8,128)(2,1)S(1)}, u32[]{:S(2)}, u32[]{:S(2)}) %collective-permute-start.5) | collective-permute-done | bytes 688160 | tf_op jit(solution)/shard_map/ppermute | solution.py:16
  79.3 3.2 collective-permute-start.6
  87.9 3.1 collective-permute-done.6
  99.1 14.9 %all-gather.6.cloned.1.call-done = bf16[512,5376]{0,1:T(8,128)(2,1)} async-done(((bf16[512,1344]{0,1:T(8,128)(2,1)}), bf16[512,5376]{0,1:T(8,128)(2,1)}) %all-gather.6.cloned.1.call-update) | async-done | bytes 5505040 | tf_op jit(solution)/shard_map/all_gather | solution.py:66
  114.0 8.1 %fusion.16 = bf16[512,512]{1,0:T(8,128)(2,1)} fusion(bf16[512,5376]{0,1:T(8,128)(2,1)} %all-gather.6.cloned.1.call-done, bf16[10752,512]{1,0:T(8,128)(2,1)} %constant_dynamic-update-slice_fusion, s32[]{:T(128)S(6)} %select_n.18), kind=kOutput, calls=%fused_computation.26 | convolution fusion | flops 2818834432 | bytes 11534340 | tf_op jit(solution)/shard_map/dot_general | solution.py:78
  122.2 4.3 %collective-permute-start.7 = (bf16[512,512]{1,0:T(8,128)(2,1)}, bf16[512,512]{1,0:T(8,128)(2,1)}, u32[]{:S(2)}, u32[]{:S(2)}) collective-permute-start(bf16[512,512]{1,0:T(8,128)(2,1)} %fusion.16), channel_id=1, source_target_pairs={{0,8},{4,12},{8,16},{12,20},{16,24},{20,28},{1,9},{5,13},{9,17},{1... | collective-permute-start | bytes 1572872 | tf_op jit(solution)/shard_map/ppermute | solution.py:25
  126.5 2.5 collective-permute-start.8
  128.9 36.2 %all-gather.8.cloned.1.call-done = bf16[5376,512]{1,0:T(8,128)(2,1)} async-done(((bf16[672,512]{1,0:T(8,128)(2,1)}), bf16[5376,512]{1,0:T(8,128)(2,1)}) %all-gather.8.cloned.1.call-update) | async-done | bytes 5505040 | tf_op jit(solution)/shard_map/all_gather | solution.py:75
  165.1 6.7 %multiply_reduce_fusion.1 = (f32[512,4]{0,1:T(4,128)S(1)}, f32[512,512]{0,1:T(8,128)S(1)}) fusion(bf16[512,5376]{0,1:T(8,128)(2,1)} %all-gather.6.cloned.1.call-done, bf16[5376,512]{1,0:T(8,128)(2,1)} %all-gather.8.cloned.1.call-done), kind=kOutput, calls=%fused_computation.32 | convolution fusion | flops 2819094528 | bytes 12066816 | tf_op jit(solution)/shard_map/dot_general | solution.py:73
  173.5 3.1 collective-permute-start.9
  176.6 2.7 collective-permute-start.10
  184.3 14.5 %collective-permute-done.9 = bf16[512,512]{0,1:T(8,128)(2,1)} collective-permute-done((bf16[512,512]{0,1:T(8,128)(2,1)S(1)}, bf16[512,512]{0,1:T(8,128)(2,1)}, u32[]{:S(2)}, u32[]{:S(2)}) %collective-permute-start.9) | collective-permute-done | bytes 524320 | tf_op jit(solution)/shard_map/ppermute | solution.py:25
  202.9 42.4 %all-gather.10.cloned.1.call-done = bf16[5376,1024]{1,0:T(8,128)(2,1)} async-done(((bf16[672,1024]{1,0:T(8,128)(2,1)}), bf16[5376,1024]{1,0:T(8,128)(2,1)}) %all-gather.10.cloned.1.call-update) | async-done | bytes 11010064 | tf_op jit(solution)/shard_map/all_gather | solution.py:70
  245.3 10.3 %convolution_bitcast_fusion = f32[64,8,8,128]{3,1,2,0:T(8,128)S(1)} fusion(bf16[512,5376]{0,1:T(8,128)(2,1)} %all-gather.6.cloned.1.call-done, bf16[5376,1024]{1,0:T(8,128)(2,1)} %all-gather.10.cloned.1.call-done), kind=kOutput, calls=%fused_computation.21 | convolution fusion | flops 5637144576 | bytes 18612224 | tf_op jit(solution)/shard_map/dot_general | solution.py:68
  259.0 11.8 %fusion.19 = f32[4,1536,512,2]{2,1,3,0:T(8,128)} fusion(bf16[512,4,128]{2,0,1:T(8,128)(2,1)S(1)} %maximum_convert_fusion, bf16[512,4,128]{2,0,1:T(8,128)(2,1)S(1)} %copy-done.5, bf16[512,4,128]{2,0,1:T(8,128)(2,1)S(1)} %copy-done.3, bf16[512,4,2,64]{3,0,2,1:T(8,128)(2,1)S(1)} %bitcast.54, bf16[512,4,2,64]{3,0,2,1:T(8,128)(2,1)S(1)} %bitcast.52), kind=kOutput, calls=%fused_computation.33 | convolution fusion | flops 1617428480 | bytes 27787264 | tf_op jit(solution)/shard_map/bhgd,khd->hgbk/dot_general | solution.py:51
  270.9 10.8 %fusion.32 = f32[4,2,512]{2,1,0:T(2,128)S(1)} fusion(pred[512,1536]{0,1:T(8,128)(4,1)} %fusion.11, bf16[512,4,128]{2,0,1:T(8,128)(2,1)S(1)} %maximum_convert_fusion, bf16[512,4,128]{2,0,1:T(8,128)(2,1)} %copy.33, bf16[512,4,128]{2,0,1:T(8,128)(2,1)S(1)} %copy-done.4, bf16[512,4,2,64]{3,0,2,1:T(8,128)(2,1)S(1)} %bitcast.55, ...), kind=kOutput, calls=%fused_computation.67 | convolution fusion | flops 1642595840 | bytes 3424256 | tf_op jit(solution)/shard_map/sub | solution.py:58
  281.6 15.4 %fusion.12 = bf16[4,128,2,512]{3,1,2,0:T(8,128)(2,1)} fusion(bf16[1536,4,128,1]{0,2,3,1:T(8,128)(2,1)} %bitcast.56, f32[4,2,512]{2,1,0:T(2,128)S(1)} %fusion.32, f32[4,1536,512,2]{2,1,3,0:T(8,128)} %fusion.19, pred[512,1536]{0,1:T(8,128)(4,1)} %fusion.11), kind=kOutput, calls=%fused_computation.24 | convolution fusion | flops 1642599936 | bytes 28590080 | tf_op jit(solution)/shard_map/hgbk,khd->bhgd/dot_general | solution.py:60
  297.1 17.6 %all-gather.14.cloned.1.call-done = bf16[4096,1344]{0,1:T(8,128)(2,1)} async-done(((bf16[512,1344]{0,1:T(8,128)(2,1)}), bf16[4096,1344]{0,1:T(8,128)(2,1)}) %all-gather.14.cloned.1.call-update) | async-done | bytes 11010064 | tf_op jit(solution)/shard_map/all_gather | solution.py:107
  314.6 82.2 %all-gather.12.cloned.1.call-done = bf16[512,4096]{0,1:T(8,128)(2,1)} async-done(((bf16[512,1024]{0,1:T(8,128)(2,1)}), bf16[512,4096]{0,1:T(8,128)(2,1)}) %all-gather.12.cloned.1.call-update) | async-done | bytes 4194320 | tf_op jit(solution)/shard_map/all_gather | solution.py:103
  396.9 10.7 %convolution_convert_fusion = bf16[512,1344]{0,1:T(8,128)(2,1)} fusion(bf16[4096,1344]{0,1:T(8,128)(2,1)} %all-gather.14.cloned.1.call-done, bf16[512,4096]{0,1:T(8,128)(2,1)} %all-gather.12.cloned.1.call-done), kind=kOutput, calls=%fused_computation.16 | convolution fusion | flops 5637832704 | bytes 16580608 | tf_op jit(solution)/shard_map/dot_general | solution.py:105
  (70 shorter events, 32.3 us)
Async XLA Ops:
  6.5 107.5 %all-gather.6.cloned.1.call-start = ((), (), s32[]{:S(2)}) async-start(), calls=%async_computation | async-start | bytes 6881280 | tf_op jit(solution)/shard_map/all_gather | solution.py:66
  7.3 157.9 %all-gather.8.cloned.1.call-start = ((), (), s32[]{:S(2)}) async-start(), calls=%async_computation.1 | async-start | bytes 6193152 | tf_op jit(solution)/shard_map/all_gather | solution.py:75
  8.0 237.3 %all-gather.10.cloned.1.call-start = ((), (), s32[]{:S(2)}) async-start(), calls=%async_computation.2 | async-start | bytes 12386304 | tf_op jit(solution)/shard_map/all_gather | solution.py:70
  8.7 305.9 %all-gather.14.cloned.1.call-start = ((), (), s32[]{:S(2)}) async-start(), calls=%async_computation.4 | async-start | bytes 12386304 | tf_op jit(solution)/shard_map/all_gather | solution.py:107
  9.3 387.5 %all-gather.12.cloned.1.call-start = ((), (), s32[]{:S(2)}) async-start(), calls=%async_computation.3 | async-start | bytes 5242880 | tf_op jit(solution)/shard_map/all_gather | solution.py:103
  9.4 12.2 %collective-permute-start = (bf16[672,512]{1,0:T(8,128)(2,1)}, bf16[672,512]{1,0:T(8,128)(2,1)S(1)}, u32[]{:S(2)}, u32[]{:S(2)}) collective-permute-start(bf16[672,512]{1,0:T(8,128)(2,1)} %param.10), channel_id=1, source_target_pairs={{0,28},{4,0},{8,4},{12,8},{16,12},{20,16},{24,20},{28,24},{1,29},{... | collective-permute-start | bytes 2064392 | tf_op jit(solution)/shard_map/ppermute | solution.py:16
  21.5 11.2 %collective-permute-start.1 = (bf16[672,512]{1,0:T(8,128)(2,1)S(1)}, bf16[672,512]{1,0:T(8,128)(2,1)S(1)}, u32[]{:S(2)}, u32[]{:S(2)}) collective-permute-start(bf16[672,512]{1,0:T(8,128)(2,1)S(1)} %collective-permute-done), channel_id=1, source_target_pairs={{0,28},{4,0},{8,4},{12,8},{16,12},{20,16},{24,20},{28,24},{1,29},{... | collective-permute-start | bytes 2064392 | tf_op jit(solution)/shard_map/ppermute | solution.py:16
  32.7 11.7 %collective-permute-start.2 = (bf16[672,512]{1,0:T(8,128)(2,1)S(1)}, bf16[672,512]{1,0:T(8,128)(2,1)S(1)}, u32[]{:S(2)}, u32[]{:S(2)}) collective-permute-start(bf16[672,512]{1,0:T(8,128)(2,1)S(1)} %collective-permute-done.1), channel_id=1, source_target_pairs={{0,28},{4,0},{8,4},{12,8},{16,12},{20,16},{24,20},{28,24},{1,29},{... | collective-permute-start | bytes 2064392 | tf_op jit(solution)/shard_map/ppermute | solution.py:16
  44.3 11.7 %collective-permute-start.3 = (bf16[672,512]{1,0:T(8,128)(2,1)S(1)}, bf16[672,512]{1,0:T(8,128)(2,1)S(1)}, u32[]{:S(2)}, u32[]{:S(2)}) collective-permute-start(bf16[672,512]{1,0:T(8,128)(2,1)S(1)} %collective-permute-done.2), channel_id=1, source_target_pairs={{0,28},{4,0},{8,4},{12,8},{16,12},{20,16},{24,20},{28,24},{1,29},{... | collective-permute-start | bytes 2064392 | tf_op jit(solution)/shard_map/ppermute | solution.py:16
  56.0 11.7 %collective-permute-start.4 = (bf16[672,512]{1,0:T(8,128)(2,1)S(1)}, bf16[672,512]{1,0:T(8,128)(2,1)S(1)}, u32[]{:S(2)}, u32[]{:S(2)}) collective-permute-start(bf16[672,512]{1,0:T(8,128)(2,1)S(1)} %collective-permute-done.3), channel_id=1, source_target_pairs={{0,28},{4,0},{8,4},{12,8},{16,12},{20,16},{24,20},{28,24},{1,29},{... | collective-permute-start | bytes 2064392 | tf_op jit(solution)/shard_map/ppermute | solution.py:16
  67.7 11.7 %collective-permute-start.5 = (bf16[672,512]{1,0:T(8,128)(2,1)S(1)}, bf16[672,512]{1,0:T(8,128)(2,1)S(1)}, u32[]{:S(2)}, u32[]{:S(2)}) collective-permute-start(bf16[672,512]{1,0:T(8,128)(2,1)S(1)} %collective-permute-done.4), channel_id=1, source_target_pairs={{0,28},{4,0},{8,4},{12,8},{16,12},{20,16},{24,20},{28,24},{1,29},{... | collective-permute-start | bytes 2064392 | tf_op jit(solution)/shard_map/ppermute | solution.py:16
  70.9 21.0 %copy-start = (bf16[672,512]{1,0:T(8,128)(2,1)S(1)}, bf16[672,512]{1,0:T(8,128)(2,1)}, u32[]{:S(2)}) copy-start(bf16[672,512]{1,0:T(8,128)(2,1)} %param.10) | copy-start | bytes 2064388
  79.3 11.7 %collective-permute-start.6 = (bf16[672,512]{1,0:T(8,128)(2,1)S(1)}, bf16[672,512]{1,0:T(8,128)(2,1)S(1)}, u32[]{:S(2)}, u32[]{:S(2)}) collective-permute-start(bf16[672,512]{1,0:T(8,128)(2,1)S(1)} %collective-permute-done.5), channel_id=1, source_target_pairs={{0,28},{4,0},{8,4},{12,8},{16,12},{20,16},{24,20},{28,24},{1,29},{... | collective-permute-start | bytes 2064392 | tf_op jit(solution)/shard_map/ppermute | solution.py:16
  122.2 50.1 %copy-start.6 = (f32[128]{0:T(128)S(1)}, f32[128]{0:T(128)}, u32[]{:S(2)}) copy-start(f32[128]{0:T(128)} %param.13) | copy-start | bytes 1540
  122.2 50.4 %copy-start.1 = (f32[512,64]{1,0:T(8,128)S(1)}, f32[512,64]{1,0:T(8,128)}, u32[]{:S(2)}) copy-start(f32[512,64]{1,0:T(8,128)} %get-tuple-element.9) | copy-start | bytes 393220
  122.2 50.4 %copy-start.2 = (f32[512,64]{1,0:T(8,128)S(1)}, f32[512,64]{1,0:T(8,128)}, u32[]{:S(2)}) copy-start(f32[512,64]{1,0:T(8,128)} %get-tuple-element.10) | copy-start | bytes 393220
  122.2 59.1 %collective-permute-start.7 = (bf16[512,512]{1,0:T(8,128)(2,1)}, bf16[512,512]{1,0:T(8,128)(2,1)}, u32[]{:S(2)}, u32[]{:S(2)}) collective-permute-start(bf16[512,512]{1,0:T(8,128)(2,1)} %fusion.16), channel_id=1, source_target_pairs={{0,8},{4,12},{8,16},{12,20},{16,24},{20,28},{1,9},{5,13},{9,17},{1... | collective-permute-start | bytes 1572872 | tf_op jit(solution)/shard_map/ppermute | solution.py:25
  126.5 54.8 %collective-permute-start.8 = (bf16[512,512]{1,0:T(8,128)(2,1)}, bf16[512,512]{1,0:T(8,128)(2,1)}, u32[]{:S(2)}, u32[]{:S(2)}) collective-permute-start(bf16[512,512]{1,0:T(8,128)(2,1)} %fusion.16), channel_id=1, source_target_pairs={{0,4},{4,8},{8,12},{12,16},{16,20},{20,24},{24,28},{1,5},{5,9},{9,... | collective-permute-start | bytes 1572872 | tf_op jit(solution)/shard_map/ppermute | solution.py:25
  173.5 25.3 %collective-permute-start.9 = (bf16[512,512]{0,1:T(8,128)(2,1)S(1)}, bf16[512,512]{0,1:T(8,128)(2,1)}, u32[]{:S(2)}, u32[]{:S(2)}) collective-permute-start(bf16[512,512]{0,1:T(8,128)(2,1)S(1)} %bitcast.59), channel_id=1, source_target_pairs={{0,8},{4,12},{8,16},{12,20},{16,24},{20,28},{1,9},{5,13},{9,17},{1... | collective-permute-start | bytes 1572872 | tf_op jit(solution)/shard_map/ppermute | solution.py:25
  176.6 24.2 %collective-permute-start.10 = (bf16[512,512]{0,1:T(8,128)(2,1)S(1)}, bf16[512,512]{0,1:T(8,128)(2,1)}, u32[]{:S(2)}, u32[]{:S(2)}) collective-permute-start(bf16[512,512]{0,1:T(8,128)(2,1)S(1)} %bitcast.60), channel_id=1, source_target_pairs={{0,4},{4,8},{8,12},{12,16},{16,20},{20,24},{24,28},{1,5},{5,9},{9,... | collective-permute-start | bytes 1572872 | tf_op jit(solution)/shard_map/ppermute | solution.py:25
  255.5 1.4 copy-start.7
  257.8 1.2 copy-start.3
  257.8 1.2 copy-start.5
  259.0 11.8 %copy-start.4 = (bf16[512,4,128]{2,0,1:T(8,128)(2,1)S(1)}, bf16[512,4,128]{2,0,1:T(8,128)(2,1)}, u32[]{:S(2)}) copy-start(bf16[512,4,128]{2,0,1:T(8,128)(2,1)} %copy.32) | copy-start | bytes 1572868
Sparse Core Ops, SparseCore 0:
  8.9 105.0 all-gather.5
  115.9 49.1 all-gather.7
  167.0 78.1 all-gather.9
  247.0 67.6 all-gather.13
  316.1 80.7 all-gather.11
